TPU v7x, 32 devices: a whole 2x2x4 slice. The times are simulated.
32 devices in a mesh: dom: 8 (over y, x, core), seq: 4 (over z).
Axes of the slice: x: 2, y: 2, z: 4, core: 2. Of those that a mesh axis runs over, the one named last changes fastest.
Arguments:
- hidden: bfloat16 [8, 160, 3072], P('dom', 'seq'), may hold values from -6 to 6
- qkv: bfloat16 [8, 160, 12288], P('dom', 'seq'), may hold values from -10 to 10
- w_out: bfloat16 [4096, 3072], P('seq'), may hold values from -0.09375 to 0.09375
- gate: float32 [3072], replicated, may hold values from 2 to 6
- next_scale: float32 [3072], replicated, may hold values from -0.5 to 1.5
- ancestors: int32 [8], replicated, may hold values from 0 to 7, as said below
- w_next: bfloat16 [3072, 12288], P('dom', 'seq'), may hold values from -0.109375 to 0.109375
Outputs:
- next_hidden: bfloat16 [8, 160, 3072], P('dom', 'seq')
- next_qkv: bfloat16 [8, 160, 12288], P('dom', None, 'seq')
Inputs may be any that keep to these rules, and one draw needn't show every extreme that they name: `ancestors`: at least one particle p continues particle p - 1, and at least one particle p continues particle p + 8 // 2 (both counted round).
All inputs are finite; a program needn't handle non-finite values.
Results may differ from a plain program's by a relative error of at most 0.017.
Values may be sent and summed in bfloat16 or wider, within the bound.
A program may use at most 64 MiB of HBM per device.

v0:
```python
import jax
import jax.numpy as jnp
from jax import lax
from jax.sharding import PartitionSpec as P

HEAD_DIM = 128


def body(hidden, qkv, w_out, gate, next_scale, ancestors, w_next):
    tok_rows = hidden.shape[1]
    model_width = hidden.shape[2]
    regrouped = lax.all_to_all(qkv[0], "seq", split_axis=1, concat_axis=0, tiled=True)
    seq_len = regrouped.shape[0]
    local_heads = regrouped.shape[1] // (3 * HEAD_DIM)
    layout = regrouped.reshape(seq_len, local_heads, 3, HEAD_DIM)
    queries = layout[:, :, 0]
    key_rows = layout[:, :, 1]
    values = layout[:, :, 2]
    scores = jnp.einsum(
        "qhd,khd->hqk", queries, key_rows, preferred_element_type=jnp.float32
    ) * HEAD_DIM ** (-0.5)
    attn_weights = jax.nn.softmax(scores, axis=-1).astype(jnp.bfloat16)
    attended = jnp.einsum("hqk,khd->qhd", attn_weights, values, preferred_element_type=jnp.float32)
    attended = attended.astype(jnp.bfloat16).reshape(seq_len, local_heads * HEAD_DIM)
    branch = lax.psum_scatter(
        jnp.dot(attended, w_out, preferred_element_type=jnp.float32).astype(jnp.bfloat16),
        "seq",
        scatter_dimension=0,
        tiled=True,
    ).astype(jnp.float32)
    updated = (hidden[0].astype(jnp.float32) + gate * branch).astype(jnp.bfloat16)
    dom_count = lax.axis_size("dom")
    pieces = updated.reshape(tok_rows, dom_count, model_width // dom_count)
    arrived = lax.all_to_all(pieces, "dom", split_axis=1, concat_axis=1, tiled=True)
    chooser = (ancestors[:, None] == jnp.arange(dom_count, dtype=jnp.int32)[None, :]).astype(
        jnp.bfloat16
    )
    routed = jnp.einsum("tsw,ds->tdw", arrived, chooser, preferred_element_type=jnp.float32).astype(
        jnp.bfloat16
    )
    returned = lax.all_to_all(routed, "dom", split_axis=1, concat_axis=1, tiled=True)
    resampled = returned.reshape(tok_rows, model_width)
    widened = resampled.astype(jnp.float32)
    squares = jnp.mean(widened * widened, axis=-1, keepdims=True)
    normed = (widened * lax.rsqrt(squares + 1e-06) * (1.0 + next_scale)).astype(jnp.bfloat16)
    gathered = lax.all_gather(normed, "seq", axis=0, tiled=True)
    projected = jnp.dot(
        gathered,
        lax.all_gather(w_next, "dom", axis=0, tiled=True),
        preferred_element_type=jnp.float32,
    )
    return (resampled[None], projected.astype(jnp.bfloat16)[None])


def solution(mesh):
    in_specs = (
        P("dom", "seq", None),
        P("dom", "seq", None),
        P("seq", None),
        P(),
        P(),
        P(),
        P("dom", "seq"),
    )
    out_specs = (P("dom", "seq", None), P("dom", None, "seq"))
    return jax.shard_map(body, mesh=mesh, in_specs=in_specs, out_specs=out_specs, check_vma=False)
```

profile of v0, /device:TPU:9, one launch (start us, length us, event | category | flops | bytes accessed | tf_op | source)
XLA Modules:
  0.0 169.8 jit_solution(11947566307316925332)
XLA Ops:
  8.0 0.0 reduce-scatter.2.cloned.1.call-start
  8.0 2.6 %all_to_all.18 = bf16[40,4,3072]{2,1,0:T(4,128)(2,1)S(1)} reshape(bf16[1,40,12288]{2,1,0:T(8,128)(2,1)} %param.8) | data formatting | bytes 1966080 | tf_op jit(solution)/shard_map/all_to_all | solution.py:12
  10.7 0.3 copy.25
  11.0 26.6 %all_to_all.26 = bf16[40,4,3072]{2,0,1:T(8,128)(2,1)S(1)} all-to-all(bf16[40,4,3072]{2,0,1:T(8,128)(2,1)S(1)} %copy.25), channel_id=1, replica_groups=mesh['dom'=8,'seq'=4] {'seq'}, dimensions={1} | all-to-all | bytes 1966080 | tf_op jit(solution)/shard_map/all_to_all | solution.py:12
  37.5 1.4 reshape.36
  38.9 1.4 fusion.16
  40.3 0.6 fusion.17
  40.9 0.5 fusion.4
  41.4 5.0 %convolution_convert_fusion.1 = bf16[160,3072]{1,0:T(8,128)(2,1)} fusion(bf16[1024,3072]{1,0:T(8,128)(2,1)} %param.9, bf16[8,20,8,128]{3,2,1,0:T(8,128)(2,1)S(1)} %fusion.4), kind=kOutput, calls=%fused_computation.2 | convolution fusion | flops 1007124480 | bytes 7602176 | tf_op jit(solution)/shard_map/dot_general | solution.py:26
  46.4 0.0 all-gather.2.cloned.1.call-start
  46.5 0.5 all-gather.2.cloned.1.call-update
  47.0 24.7 %reduce-scatter.2.cloned.1.call-done = bf16[40,3072]{1,0:T(8,128)(2,1)} async-done(((bf16[160,3072]{1,0:T(8,128)(2,1)}), bf16[40,3072]{1,0:T(8,128)(2,1)}) %reduce-scatter.2.cloned.1.call-update) | async-done | bytes 245776 | tf_op jit(solution)/shard_map/reduce_scatter | solution.py:25
  71.8 1.0 fusion.7
  72.8 11.2 %all_to_all.27 = bf16[40,8,384]{2,0,1:T(8,128)(2,1)S(1)} all-to-all(bf16[40,8,384]{2,0,1:T(8,128)(2,1)S(1)} %bitcast.51), channel_id=1, replica_groups=mesh['dom'=8,'seq'=4] {'dom'}, dimensions={1} | all-to-all | bytes 491520 | tf_op jit(solution)/shard_map/all_to_all | solution.py:34
  84.1 0.3 fusion.5
  84.3 0.7 copy.33
  85.1 6.4 %all-to-all-start.2 = ((bf16[40,8,384]{2,0,1:T(8,128)(2,1)}), bf16[40,8,384]{2,0,1:T(8,128)(2,1)S(1)}, u32[]{:S(2)}, u32[]{:S(2)}) async-start(bf16[40,8,384]{2,0,1:T(8,128)(2,1)} %copy.33), calls=%async_computation.3 | async-start | bytes 491520 | tf_op jit(solution)/shard_map/all_to_all | solution.py:41
  91.5 5.6 %all-to-all-done.2 = bf16[40,8,384]{2,0,1:T(8,128)(2,1)S(1)} async-done(((bf16[40,8,384]{2,0,1:T(8,128)(2,1)}), bf16[40,8,384]{2,0,1:T(8,128)(2,1)S(1)}, u32[]{:S(2)}, u32[]{:S(2)}) %all-to-all-start.2) | async-done | bytes 245792 | tf_op jit(solution)/shard_map/all_to_all | solution.py:41
  97.2 0.8 broadcast_in_dim_reshape.3
  98.1 0.2 fusion.6
  98.2 0.1 multiply_convert_fusion
  98.4 17.7 %all_gather.6 = bf16[160,3072]{1,0:T(8,128)(2,1)S(1)} all-gather(bf16[40,3072]{1,0:T(8,128)(2,1)S(1)} %multiply_convert_fusion), channel_id=1, replica_groups=mesh['dom'=8,'seq'=4] {'seq'}, dimensions={0}, use_global_device_ids=true | all-gather | bytes 1228800 | tf_op jit(solution)/shard_map/all_gather | solution.py:46
  116.1 35.7 %all-gather.2.cloned.1.call-done = bf16[3072,3072]{1,0:T(8,128)(2,1)} async-done(((bf16[384,3072]{1,0:T(8,128)(2,1)}), bf16[3072,3072]{1,0:T(8,128)(2,1)}) %all-gather.2.cloned.1.call-update) | async-done | bytes 18874384 | tf_op jit(solution)/shard_map/all_gather | solution.py:49
  151.8 10.5 %fusion.1 = bf16[1,160,3072]{2,1,0:T(8,128)(2,1)} fusion(bf16[160,3072]{1,0:T(8,128)(2,1)S(1)} %all_gather.6, bf16[3072,3072]{1,0:T(8,128)(2,1)} %all-gather.2.cloned.1.call-done), kind=kOutput, calls=%fused_computation.3 | convolution fusion | flops 3020390400 | bytes 20840448 | tf_op jit(solution)/shard_map/dot_general | solution.py:47
  (15 shorter events, 0.2 us)
Async XLA Ops:
  8.0 63.8 %reduce-scatter.2.cloned.1.call-start = ((), (), s32[]{:S(2)}) async-start(), calls=%async_computation.4 | async-start | bytes 1228800 | tf_op jit(solution)/shard_map/reduce_scatter | solution.py:25
  46.4 25.4 %copy-start = (bf16[1,40,3072]{2,1,0:T(8,128)(2,1)S(1)}, bf16[1,40,3072]{2,1,0:T(8,128)(2,1)}, u32[]{:S(2)}) copy-start(bf16[1,40,3072]{2,1,0:T(8,128)(2,1)} %param.7) | copy-start | bytes 737284
  46.4 25.3 %copy-start.2 = (f32[3072]{0:T(1024)S(1)}, f32[3072]{0:T(1024)}, u32[]{:S(2)}) copy-start(f32[3072]{0:T(1024)} %param.10) | copy-start | bytes 36868
  46.4 105.4 %all-gather.2.cloned.1.call-start = ((), (), s32[]{:S(2)}) async-start(), calls=%async_computation.5 | async-start | bytes 21233664 | tf_op jit(solution)/shard_map/all_gather | solution.py:49
  47.0 37.0 %copy-start.3 = (s32[8]{0:T(128)S(1)}, s32[8]{0:T(128)}, u32[]{:S(2)}) copy-start(s32[8]{0:T(128)} %param.12) | copy-start | bytes 100
  72.8 18.7 %copy-start.1 = (f32[3072]{0:T(1024)S(1)}, f32[3072]{0:T(1024)}, u32[]{:S(2)}) copy-start(f32[3072]{0:T(1024)} %param.11) | copy-start | bytes 36868
  85.1 12.1 %all-to-all-start.2 = ((bf16[40,8,384]{2,0,1:T(8,128)(2,1)}), bf16[40,8,384]{2,0,1:T(8,128)(2,1)S(1)}, u32[]{:S(2)}, u32[]{:S(2)}) async-start(bf16[40,8,384]{2,0,1:T(8,128)(2,1)} %copy.33), calls=%async_computation.3 | async-start | bytes 491520 | tf_op jit(solution)/shard_map/all_to_all | solution.py:41
Sparse Core Ops, SparseCore 0:
  46.5 25.1 reduce-scatter.1
Sparse Core Ops, SparseCore 1:
  48.8 103.0 all-gather.1
where the time goes:
time: 172 us; the launch traced here: 170 us
  waiting for transfers between devices  66.6 us (39%)
  blocking collectives  55.5 us (32%)
  matrix products  16.8 us (10%)
  between operations  15.6 us (9%)
  local copies, waits for them, and re-layouts  7.38 us (4%)
  starting transfers between devices  6.51 us (4%)
    all_gather x1, waiting for transfers between devices, body(): lax.all_gather(w_next, 'dom', axis=0, tiled=True)  35.7 us
    all_to_all x1, blocking collectives, body(): lax.all_to_all(qkv[0], 'seq', split_axis=1, concat_axis=0, tiled=True)  26.6 us
    reduce_scatter x1, waiting for transfers between devices, body(): lax.psum_scatter(jnp.dot(attended, w_out, preferred_element_type=jnp.floa...  24.7 us
    all_gather x1, blocking collectives, body(): gathered = lax.all_gather(normed, 'seq', axis=0, tiled=True)  17.7 us
    all_to_all x1, blocking collectives, body(): lax.all_to_all(pieces, 'dom', split_axis=1, concat_axis=1, tiled=True)  11.2 us
    dot_general x1, matrix products, body(): jnp.dot(gathered, lax.all_gather(w_next, 'dom', axis=0, tiled=True), pref...  10.5 us
    all_to_all x1, starting transfers between devices, body(): lax.all_to_all(routed, 'dom', split_axis=1, concat_axis=1, tiled=True)  6.43 us
    all_to_all x1, waiting for transfers between devices, body(): lax.all_to_all(routed, 'dom', split_axis=1, concat_axis=1, tiled=True)  5.62 us
  transfers between devices with their start and end apart: 3, of which 3 were waited for; matrix products, arithmetic and copies ran while one was open for 2% of the time, Pallas kernels for 0%

commit v1 on v0

v1 whole, which is shorter than its diff:
```python
import functools

import jax
import jax.numpy as jnp
from jax import lax
from jax.experimental import pallas as pl
from jax.experimental.pallas import tpu as pltpu
from jax.sharding import PartitionSpec as P

HEAD_DIM = 128
MESH = pl.DeviceIdType.MESH
F32 = jnp.float32
BF16 = jnp.bfloat16
OUT_CHUNKS = 2


def tile_of(width, most):
    return max(t for t in range(128, most + 1, 128) if width % t == 0)


def kernel(
    dom_n, seq_n,
    anc_ref, hidden_ref, qkv_ref, wout_ref, gate_ref, scale_ref, wnext_ref,
    nh_ref, out_ref,
    heads, wout_v, hid_v, att, part, rs_in, pieces, arrived, routed, landed,
    normed, act, w_all, acc,
    loc_sem, qs, qr, rs_s, rs_r, a_s, a_r, b_s, b_r, n_s, n_r,
    ring_s, ring_r, mate_s, mate_r, own_s, own_r,
):
    d = lax.axis_index("dom")
    s = lax.axis_index("seq")
    rows, width = hid_v.shape
    seq_len = seq_n * rows
    chips = dom_n // 2
    core = lax.rem(d, 2)
    mate = d + 1 - 2 * core
    chip = d // 2

    if chips % 2 == 0:
        half_n = chips // 2

        def chip_at(pos):
            back = pos // half_n
            return (1 - back) * 2 * pos + back * (2 * (chips - 1 - pos) + 1)

        pos = chip // 2 + lax.rem(chip, 2) * (chips - 1 - 2 * (chip // 2))
    else:
        def chip_at(pos):
            return pos

        pos = chip

    def at(offset):
        return chip_at(lax.rem(pos + offset + 2 * chips, chips))

    barrier = pltpu.get_barrier_semaphore()
    for k in range(1, seq_n):
        pl.semaphore_signal(barrier, inc=1, device_id=(d, lax.rem(s + k, seq_n)), device_id_type=MESH)
    for k in range(1, dom_n):
        pl.semaphore_signal(barrier, inc=1, device_id=(lax.rem(d + k, dom_n), s), device_id_type=MESH)
    pl.semaphore_wait(barrier, seq_n - 1 + dom_n - 1)

    def push(src, dst, send, recv, dev):
        return pltpu.make_async_remote_copy(
            src_ref=src, dst_ref=dst, send_sem=send, recv_sem=recv, device_id=dev, device_id_type=MESH
        )

    sent = []

    cols = heads.shape[2]
    q_copies = []
    order = sorted(range(1, seq_n), key=lambda k: -min(k, seq_n - k))
    for k in order:
        to = lax.rem(s + k, seq_n)
        c = push(
            qkv_ref.at[0, :, pl.ds(pl.multiple_of(to * cols, 128), cols)],
            heads.at[s], qs.at[k], qr.at[k], (d, to),
        )
        c.start()
        q_copies.append(c)
    sent += q_copies

    wrows = wnext_ref.shape[0]
    wcols = wnext_ref.shape[1] // 2

    def slot(half, owner):
        return w_all.at[half, pl.ds(pl.multiple_of(owner * wrows, 16), wrows), :]

    def ring(h, half):
        step = 1 if half == 0 else -1
        owner = 2 * at(-step * h) + core
        if h == 0:
            src = wnext_ref.at[:, pl.ds(half * wcols, wcols)]
        else:
            src = slot(half, owner)
        return push(
            src, slot(half, owner), ring_s.at[h, half], ring_r.at[h, half],
            (2 * at(step) + core, s),
        )

    def mate_copy(h, half):
        step = 1 if half == 0 else -1
        owner = 2 * at(-step * (h + 1)) + core
        return push(
            slot(half, owner), slot(half, owner), mate_s.at[h, half], mate_r.at[h, half], (mate, s)
        )

    hops = chips - 1
    ring_copies = {}
    mate_copies = {}

    def start_ring(h):
        for half in range(2):
            ring_copies[h, half] = ring(h, half)
            ring_copies[h, half].start()
            sent.append(ring_copies[h, half])

    def arrive(h):
        for half in range(2):
            ring_copies[h, half].wait_recv()

    def share(h):
        for half in range(2):
            mate_copies[h, half] = mate_copy(h, half)
            mate_copies[h, half].start()
            sent.append(mate_copies[h, half])

    if hops > 0:
        start_ring(0)
    own_copies = []
    local = []
    for half in range(2):
        src = wnext_ref.at[:, pl.ds(half * wcols, wcols)]
        c = push(src, slot(half, d), own_s.at[half], own_r.at[half], (mate, s))
        c.start()
        own_copies.append(c)
    sent += own_copies

    def keep(src, dst, i):
        c = pltpu.make_async_copy(src, dst, loc_sem.at[i])
        c.start()
        return c

    own_heads = keep(qkv_ref.at[0, :, pl.ds(pl.multiple_of(s * cols, 128), cols)], heads.at[s], 0)
    wout_copy = keep(wout_ref, wout_v, 1)
    hid_copy = keep(hidden_ref.at[0], hid_v, 2)
    own_w = [
        keep(wnext_ref.at[:, pl.ds(half * wcols, wcols)], slot(half, d), 3 + half) for half in range(2)
    ]

    own_heads.wait()
    for c in q_copies:
        c.wait_recv()

    done_hop = 0
    if hops > 0:
        arrive(0)
        if hops > 1:
            start_ring(1)
        share(0)

    head_n = cols // (3 * HEAD_DIM)

    def merge(x):
        return x.astype(F32).reshape(seq_len, x.shape[-1]).astype(BF16)

    def one_head(h, carry):
        base = pl.multiple_of(h * 3 * HEAD_DIM, HEAD_DIM)
        q = merge(heads[:, :, pl.ds(base, HEAD_DIM)])
        key = merge(heads[:, :, pl.ds(pl.multiple_of(base + HEAD_DIM, HEAD_DIM), HEAD_DIM)])
        v = merge(heads[:, :, pl.ds(pl.multiple_of(base + 2 * HEAD_DIM, HEAD_DIM), HEAD_DIM)])
        sc = lax.dot_general(q, key, (((1,), (1,)), ((), ())), preferred_element_type=F32)
        sc = sc * HEAD_DIM ** (-0.5)
        e = jnp.exp(sc - jnp.max(sc, axis=-1, keepdims=True))
        w = (e / jnp.sum(e, axis=-1, keepdims=True)).astype(BF16)
        o = jnp.dot(w, v, preferred_element_type=F32).astype(BF16)
        att[:, pl.ds(pl.multiple_of(h * HEAD_DIM, HEAD_DIM), HEAD_DIM)] = o
        return carry

    lax.fori_loop(0, head_n, one_head, 0)
    wout_copy.wait()

    chunk = width // OUT_CHUNKS
    tile = tile_of(chunk, 512)
    rs_copies = []
    for n in range(OUT_CHUNKS):
        def project(t, carry, n=n):
            c0 = pl.ds(pl.multiple_of(n * chunk + t * tile, 128), tile)
            y = jnp.dot(att[...], wout_v[:, c0], preferred_element_type=F32)
            part[:, :, c0] = y.reshape(seq_n, rows, tile).astype(BF16)
            return carry

        lax.fori_loop(0, chunk // tile, project, 0)
        for k in order:
            to = lax.rem(s + k, seq_n)
            c = push(
                part.at[to, :, pl.ds(n * chunk, chunk)], rs_in.at[s, :, pl.ds(n * chunk, chunk)],
                rs_s.at[n, k], rs_r.at[n, k], (d, to),
            )
            c.start()
            rs_copies.append(c)
    sent += rs_copies
    hid_copy.wait()

    if hops > 1:
        arrive(1)
        share(1)
    for c in rs_copies:
        c.wait_recv()

    piece = width // dom_n
    for j in range(dom_n):
        c0 = slice(j * piece, (j + 1) * piece)
        total = part[s, :, c0].astype(F32)
        for k in range(1, seq_n):
            total = total + rs_in[lax.rem(s + k, seq_n), :, c0].astype(F32)
        pieces[j] = (hid_v[:, c0].astype(F32) + gate_ref[:, c0] * total).astype(BF16)

    a_copies = []
    for k in range(1, dom_n):
        to = lax.rem(d + k, dom_n)
        c = push(pieces.at[to], arrived.at[d], a_s.at[k], a_r.at[k], (to, s))
        c.start()
        a_copies.append(c)
    sent += a_copies
    arrived[d] = pieces[d]
    for c in a_copies:
        c.wait_recv()
    for p in range(dom_n):
        routed[p] = arrived[anc_ref[p]]
    b_copies = []
    for k in range(1, dom_n):
        to = lax.rem(d + k, dom_n)
        c = push(routed.at[to], landed.at[d], b_s.at[k], b_r.at[k], (to, s))
        c.start()
        b_copies.append(c)
    sent += b_copies
    landed[d] = routed[d]
    for c in b_copies:
        c.wait_recv()
    if hops > 2:
        start_ring(2)

    squares = jnp.zeros((rows, 1), F32)
    for j in range(dom_n):
        x = landed[j]
        nh_ref[0, :, j * piece:(j + 1) * piece] = x
        x = x.astype(F32)
        squares = squares + jnp.sum(x * x, axis=-1, keepdims=True)
    inv = lax.rsqrt(squares / width + 1e-06)
    for j in range(dom_n):
        c0 = slice(j * piece, (j + 1) * piece)
        normed[s, :, c0] = (landed[j].astype(F32) * inv * (1.0 + scale_ref[:, c0])).astype(BF16)
    n_copies = []
    for k in order:
        to = lax.rem(s + k, seq_n)
        c = push(normed.at[s], normed.at[s], n_s.at[k], n_r.at[k], (d, to))
        c.start()
        n_copies.append(c)
    sent += n_copies
    for c in own_w:
        c.wait()
    for c in own_copies:
        c.wait_recv()
    for c in n_copies:
        c.wait_recv()
    act[...] = merge(normed[...])

    wide = tile_of(wcols, 512)
    steps = wcols // wide
    aligned = wrows % 128 == 0

    def add(half, owner, first, last):
        k0 = pl.multiple_of(owner * wrows, 128)

        def body(t, carry):
            c0 = pl.ds(pl.multiple_of(t * wide, 128), wide)
            o0 = pl.ds(pl.multiple_of(half * wcols + t * wide, 128), wide)
            y = jnp.dot(
                act[:, pl.ds(k0, wrows)], w_all[half, pl.ds(k0, wrows), c0],
                preferred_element_type=F32,
            )
            if not first:
                y = y + acc[:, o0]
            if last:
                out_ref[0, :, o0] = y.astype(BF16)
            else:
                acc[:, o0] = y
            return carry

        lax.fori_loop(0, steps, body, 0)

    if aligned:
        for half in range(2):
            add(half, d, True, False)
            add(half, mate, False, hops == 0)
    for h in range(hops):
        if h > 1:
            arrive(h)
            if h + 1 < hops:
                start_ring(h + 1)
            share(h)
        last = h == hops - 1
        for half in range(2):
            step = 1 if half == 0 else -1
            if aligned:
                add(half, 2 * at(-step * (h + 1)) + core, False, False)
        for half in range(2):
            step = 1 if half == 0 else -1
            mate_copies[h, half].wait_recv()
            if aligned:
                add(half, 2 * at(-step * (h + 1)) + 1 - core, False, last)
    if not aligned:
        for half in range(2):
            def whole(t, carry, half=half):
                c0 = pl.ds(pl.multiple_of(t * wide, 128), wide)
                o0 = pl.ds(pl.multiple_of(half * wcols + t * wide, 128), wide)
                y = jnp.dot(act[...], w_all[half, :, c0], preferred_element_type=F32)
                out_ref[0, :, o0] = y.astype(BF16)
                return carry

            lax.fori_loop(0, steps, whole, 0)
    for c in sent:
        c.wait_send()


def body(dom_n, seq_n, hidden, qkv, w_out, gate, next_scale, ancestors, w_next):
    _, rows, width = hidden.shape
    cols = qkv.shape[2] // seq_n
    seq_len = rows * seq_n
    out_cols = w_next.shape[1]
    att_cols = w_out.shape[0]
    hops = max(dom_n // 2 - 1, 1)
    piece = width // dom_n
    sem = pltpu.SemaphoreType.DMA
    any_spec = pl.BlockSpec(memory_space=pl.ANY)
    vmem = pl.BlockSpec(memory_space=pltpu.VMEM)
    return pl.pallas_call(
        functools.partial(kernel, dom_n, seq_n),
        out_shape=(
            jax.ShapeDtypeStruct((1, rows, width), BF16),
            jax.ShapeDtypeStruct((1, seq_len, out_cols), BF16),
        ),
        in_specs=[
            pl.BlockSpec(memory_space=pltpu.SMEM), any_spec, any_spec, any_spec, vmem, vmem, any_spec,
        ],
        out_specs=(vmem, vmem),
        scratch_shapes=[
            pltpu.VMEM((seq_n, rows, cols), BF16),
            pltpu.VMEM((att_cols, width), BF16),
            pltpu.VMEM((rows, width), BF16),
            pltpu.VMEM((seq_len, att_cols), BF16),
            pltpu.VMEM((seq_n, rows, width), BF16),
            pltpu.VMEM((seq_n, rows, width), BF16),
            pltpu.VMEM((dom_n, rows, piece), BF16),
            pltpu.VMEM((dom_n, rows, piece), BF16),
            pltpu.VMEM((dom_n, rows, piece), BF16),
            pltpu.VMEM((dom_n, rows, piece), BF16),
            pltpu.VMEM((seq_n, rows, width), BF16),
            pltpu.VMEM((seq_len, width), BF16),
            pltpu.VMEM((2, width, out_cols // 2), BF16),
            pltpu.VMEM((seq_len, out_cols), F32),
            sem((5,)),
            sem((seq_n,)), sem((seq_n,)),
            sem((OUT_CHUNKS, seq_n)), sem((OUT_CHUNKS, seq_n)),
            sem((dom_n,)), sem((dom_n,)),
            sem((dom_n,)), sem((dom_n,)),
            sem((seq_n,)), sem((seq_n,)),
            sem((hops, 2)), sem((hops, 2)),
            sem((hops, 2)), sem((hops, 2)),
            sem((2,)), sem((2,)),
        ],
        compiler_params=pltpu.CompilerParams(
            collective_id=0, has_side_effects=True, vmem_limit_bytes=60 * 1024 * 1024
        ),
    )(ancestors, hidden, qkv, w_out, gate[None], next_scale[None], w_next)


def solution(mesh):
    in_specs = (
        P("dom", "seq", None),
        P("dom", "seq", None),
        P("seq", None),
        P(),
        P(),
        P(),
        P("dom", "seq"),
    )
    out_specs = (P("dom", "seq", None), P("dom", None, "seq"))
    return jax.shard_map(
        functools.partial(body, mesh.shape["dom"], mesh.shape["seq"]),
        mesh=mesh, in_specs=in_specs, out_specs=out_specs, check_vma=False,
    )
```

time: 172 us -> 111 us (0.65); the launches traced: 170 us -> 111 us
  Pallas kernels: 0 us -> 107 us
  waiting for transfers between devices: 66.6 us -> 0 us
  blocking collectives: 55.5 us -> 0 us
  matrix products: 16.8 us -> 0 us
  between operations: 15.6 us -> 0.64 us
  starting transfers between devices: 6.51 us -> 0 us
  local copies, waits for them, and re-layouts: 7.38 us -> 3.86 us
    pallas_call x0 -> x1, Pallas kernels: none -> 107 us  [body(): pl.pallas_call(functools.partial(kernel, dom_n, seq_n), out_shape=(jax.Sh...]
    all_to_all x2 -> x0, blocking collectives: 37.8 us -> none  [the longest x1 26.6 us: body(): lax.all_to_all(qkv[0], 'seq', split_axis=1, concat_axis=0, tiled=True)]
    all_gather x1 -> x0, waiting for transfers between devices: 35.7 us -> none  [body(): lax.all_gather(w_next, 'dom', axis=0, tiled=True)]
    reduce_scatter x1 -> x0, waiting for transfers between devices: 24.7 us -> none  [body(): lax.psum_scatter(jnp.dot(attended, w_out, preferred_element_type=jnp.floa...]
    all_gather x1 -> x0, blocking collectives: 17.7 us -> none  [body(): gathered = lax.all_gather(normed, 'seq', axis=0, tiled=True)]
    dot_general x4 -> x0, matrix products: 16.3 us -> none  [the longest x1 10.5 us: body(): jnp.dot(gathered, lax.all_gather(w_next, 'dom', axis=0, tiled=True), pref...]
    all_to_all x1 -> x0, starting transfers between devices: 6.43 us -> none  [body(): lax.all_to_all(routed, 'dom', split_axis=1, concat_axis=1, tiled=True)]
    all_to_all x1 -> x0, waiting for transfers between devices: 5.62 us -> none  [body(): lax.all_to_all(routed, 'dom', split_axis=1, concat_axis=1, tiled=True)]
  transfers between devices with their start and end apart: 3 -> 0, of which waited for: 3 -> 0; matrix products, arithmetic and copies ran while one was open for 2% -> 0% of each run, Pallas kernels for 0% -> 0%
where the time goes in v1:
time: 111 us
  Pallas kernels  107 us (96%)
  local copies, waits for them, and re-layouts  3.86 us (3%)
    pallas_call x1, Pallas kernels, body(): pl.pallas_call(functools.partial(kernel, dom_n, seq_n), out_shape=(jax.Sh...  107 us
    unnamed x2, local copies, waits for them, and re-layouts  3.86 us

profile of v1, /device:TPU:9, one launch (start us, length us, event | category | flops | bytes accessed | tf_op | source)
XLA Modules:
  0.0 111.1 jit_solution(16614068061138925757)
XLA Ops:
  0.6 106.6 %shard_map.86 = (bf16[1,40,3072]{2,1,0:T(8,128)(2,1)}, bf16[1,160,3072]{2,1,0:T(8,128)(2,1)}) custom-call(s32[8]{0:T(128)} %anc_ref.1, bf16[1,40,3072]{2,1,0:T(8,128)(2,1)} %hidden_ref.1, bf16[1,40,12288]{2,1,0:T(8,128)(2,1)} %qkv_ref.1, bf16[1024,3072]{1,0:T(8,128)(2,1)} %wout_ref.1, f32[1,3072]{1,0:T(1,128)} %bitcast.2, f32[1,3072]{1,0:T(1,128)} %bitcast.3, ...), custom_call_target="tpu_custom_call" | custom-call | tf_op jit(solution)/shard_map/pallas_call | solution.py:338
  107.2 1.7 %copy.11 = bf16[1,40,3072]{2,1,0:T(8,128)(2,1)} copy(bf16[1,40,3072]{2,1,0:T(8,128)(2,1)} %get-tuple-element.4) | data formatting | bytes 491520
  108.9 2.2 %copy.12 = bf16[1,160,3072]{2,1,0:T(8,128)(2,1)} copy(bf16[1,160,3072]{2,1,0:T(8,128)(2,1)} %get-tuple-element.5) | data formatting | bytes 1966080
